TPU v7x, 512 devices: a whole 4x4x16 slice. The times are simulated.
512 devices in a mesh: dp: 4 (over x), expert: 128 (over z, y, core).
Axes of the slice: x: 4, y: 4, z: 16, core: 2. Of those that a mesh axis runs over, the one named last changes fastest.
Arguments:
- tokens: bfloat16 [65536, 2048], P(('dp', 'expert')), may hold values from -6 to 6
- hidden_grad: bfloat16 [65536, 1, 768], P(('dp', 'expert')), may hold values from -6 to 6
- gate_prob: float32 [65536, 1], P(('dp', 'expert')), may hold values from 0.2 to 1
- slot_choice: int32 [65536, 1], P(('dp', 'expert')), may hold values from 0 to 127; in each aligned block of 128 rows (0 to 127, 128 to 255, ...) at most 2 rows name the same one
- replica_plan: int32 [128], replicated, may hold values from 0 to 63, as said below
- weights: bfloat16 [64, 2, 2048, 768], P(None, None, ('dp', 'expert')), may hold values from -0.125 to 0.125
Outputs:
- input_grad: bfloat16 [65536, 2048], P(('dp', 'expert'))
- expert_grad: bfloat16 [64, 2, 2048, 768], P(None, None, ('dp', 'expert'))
Inputs may be any that keep to these rules, and one draw needn't show every extreme that they name: `slot_choice`: among the tokens of one device no slot is named more than 2 times, and 2 is reached; the picks of one token name different slots. `replica_plan`: every expert is held by at least one slot.
All inputs are finite; a program needn't handle non-finite values.
Results may differ from a plain program's by a relative error of at most 0.007.
Values may be sent and summed in bfloat16 or wider, within the bound.
A program may use at most 64 MiB of HBM per device.

v0:
```python
import jax
import jax.numpy as jnp
from jax import lax
from jax.sharding import PartitionSpec as P


def back_project(grad_gate, grad_up, weight_pair):
    contract_cols = (((1,), (1,)), ((), ()))
    first_term = lax.dot_general(
        grad_gate, weight_pair[0], contract_cols, preferred_element_type=jnp.float32
    )
    return first_term + lax.dot_general(
        grad_up, weight_pair[1], contract_cols, preferred_element_type=jnp.float32
    )


def row_products(inputs, grad_gate, grad_up):
    contract_rows = (((0,), (0,)), ((), ()))
    return jnp.stack(
        [
            lax.dot_general(inputs, grad_gate, contract_rows, preferred_element_type=jnp.float32),
            lax.dot_general(inputs, grad_up, contract_rows, preferred_element_type=jnp.float32),
        ]
    )


def per_device(tokens, hidden_grad, gate_prob, slot_choice, replica_plan, weights):
    expert_count = lax.axis_size("expert")
    group_count = lax.axis_size("dp")
    token_count, pick_count = slot_choice.shape
    row_count = token_count * pick_count
    capacity = max(2, 2 * row_count // expert_count)
    depth_rows = expert_count * capacity
    model_width = tokens.shape[1]
    hidden_width = hidden_grad.shape[2]
    expert_total = weights.shape[0]
    shard_rows = weights.shape[2]
    block_rows = shard_rows * expert_count
    flat_slot = slot_choice.reshape(row_count)
    slot_member = (flat_slot[:, None] == jnp.arange(expert_count, dtype=jnp.int32)[None, :]).astype(
        jnp.int32
    )
    ranking = jnp.sum((jnp.cumsum(slot_member, axis=0) - 1) * slot_member, axis=1)
    position = flat_slot * capacity + ranking
    scatter_table = (jnp.arange(depth_rows, dtype=jnp.int32)[:, None] == position[None, :]).astype(
        jnp.bfloat16
    )
    token_rows = jnp.repeat(tokens, pick_count, axis=0)
    cotangent = (gate_prob[:, :, None] * hidden_grad.astype(jnp.float32)).astype(jnp.bfloat16)
    cotangent = cotangent.reshape(row_count, hidden_width)
    send_inputs = jnp.dot(scatter_table, token_rows, preferred_element_type=jnp.float32).astype(
        jnp.bfloat16
    )
    send_cotangent = jnp.dot(scatter_table, cotangent, preferred_element_type=jnp.float32).astype(
        jnp.bfloat16
    )
    recv_inputs, recv_cotangent = (
        lax.all_to_all(
            send_inputs.reshape(expert_count, capacity, model_width),
            "expert",
            split_axis=0,
            concat_axis=0,
            tiled=True,
        ),
        lax.all_to_all(
            send_cotangent.reshape(expert_count, capacity, hidden_width),
            "expert",
            split_axis=0,
            concat_axis=0,
            tiled=True,
        ),
    )
    recv_inputs = recv_inputs.reshape(depth_rows, model_width)
    recv_cotangent = recv_cotangent.reshape(depth_rows, hidden_width)
    chooser = (replica_plan[:, None] == jnp.arange(expert_total, dtype=jnp.int32)[None, :]).astype(
        jnp.bfloat16
    )
    send_weights = jnp.einsum(
        "se,ekdf->skdf", chooser, weights, preferred_element_type=jnp.float32
    ).astype(jnp.bfloat16)
    own_weights = lax.all_to_all(
        send_weights, "expert", split_axis=0, concat_axis=2, tiled=True
    ).reshape(2, block_rows, hidden_width)
    piece = lax.all_gather(own_weights, "dp", axis=1, tiled=True)
    gate_sum = jnp.dot(recv_inputs, piece[0], preferred_element_type=jnp.float32)
    up_sum = jnp.dot(recv_inputs, piece[1], preferred_element_type=jnp.float32)
    sigma = jax.nn.sigmoid(gate_sum)
    scaled = recv_cotangent.astype(jnp.float32)
    grad_gate = (scaled * up_sum * sigma * (1.0 + gate_sum * (1.0 - sigma))).astype(jnp.bfloat16)
    grad_up = (scaled * gate_sum * sigma).astype(jnp.bfloat16)
    all_gate, all_up = (
        lax.all_gather(grad_gate, "dp", axis=0, tiled=True),
        lax.all_gather(grad_up, "dp", axis=0, tiled=True),
    )
    split_inputs = recv_inputs.reshape(depth_rows, group_count, block_rows)
    all_columns = lax.all_to_all(
        split_inputs, "dp", split_axis=1, concat_axis=0, tiled=True
    ).reshape(group_count * depth_rows, block_rows)
    row_terms = back_project(all_gate, all_up, own_weights).astype(jnp.bfloat16)
    summed = jnp.zeros((2, block_rows, hidden_width), jnp.float32)
    for group_index in range(group_count):
        lower = group_index * depth_rows
        upper = lower + depth_rows
        products = row_products(
            all_columns[lower:upper], all_gate[lower:upper], all_up[lower:upper]
        )
        summed = summed + lax.optimization_barrier(products.astype(jnp.bfloat16)).astype(
            jnp.float32
        )
    pieces = summed.reshape(2, expert_count, shard_rows, hidden_width)
    gathered = lax.all_to_all(
        pieces.astype(jnp.bfloat16), "expert", split_axis=1, concat_axis=1, tiled=True
    ).astype(pieces.dtype)
    membership = (
        jnp.arange(expert_total, dtype=jnp.int32)[:, None] == replica_plan[None, :]
    ).astype(jnp.float32)
    expert_grad = jnp.einsum("es,ksdf->ekdf", membership, gathered, precision=lax.Precision.HIGHEST)
    expert_grad = (expert_grad / group_count).astype(jnp.bfloat16)
    joined = lax.all_to_all(
        row_terms.reshape(group_count, depth_rows, block_rows),
        "dp",
        split_axis=0,
        concat_axis=2,
        tiled=True,
    )
    back_rows = lax.all_to_all(
        joined.reshape(expert_count, capacity, model_width),
        "expert",
        split_axis=0,
        concat_axis=0,
        tiled=True,
    )
    back_rows = back_rows.reshape(depth_rows, model_width)
    token_grads = lax.dot_general(
        scatter_table, back_rows, (((0,), (0,)), ((), ())), preferred_element_type=jnp.float32
    )
    input_grad = jnp.sum(token_grads.reshape(token_count, pick_count, model_width), axis=1).astype(
        jnp.bfloat16
    )
    return (input_grad, expert_grad)


def solution(mesh):
    placed = (
        P(("dp", "expert"), None),
        P(("dp", "expert"), None, None),
        P(("dp", "expert"), None),
        P(("dp", "expert"), None),
        P(),
        P(None, None, ("dp", "expert"), None),
    )
    return jax.shard_map(
        per_device,
        mesh=mesh,
        in_specs=placed,
        out_specs=(P(("dp", "expert"), None), P(None, None, ("dp", "expert"), None)),
        check_vma=False,
    )
```

profile of v0, /device:TPU:33, one launch (start us, length us, event | category | flops | bytes accessed | tf_op | source)
XLA Modules:
  0.0 494.8 jit_solution(11595988162404496423)
XLA Ops:
  7.2 1.1 copy-done
  8.3 1.3 convolution_convert_fusion.2
  9.6 1.2 copy.26
  10.8 96.8 %all_to_all.65 = bf16[128,2,4,768]{3,2,1,0:T(4,128)(2,1)S(1)} all-to-all(bf16[128,2,4,768]{3,2,1,0:T(4,128)(2,1)S(1)} %copy.26), channel_id=1, replica_groups=mesh['dp'=4,'expert'=128] {'expert'}, dimensions={0} | all-to-all | bytes 3145728 | tf_op jit(solution)/shard_map/all_to_all | solution.py:81
  107.6 2.4 copy.27
  110.0 0.6 copy-done.7
  111.4 0.9 reshape.66
  112.3 7.0 %all-to-all-start = ((bf16[128,2,768]{2,1,0:T(2,128)(2,1)}), bf16[128,2,768]{2,1,0:T(2,128)(2,1)S(1)}, u32[]{:S(2)}, u32[]{:S(2)}) async-start(bf16[128,2,768]{2,1,0:T(2,128)(2,1)} %reshape.66), calls=%async_computation | async-start | bytes 786432 | tf_op jit(solution)/shard_map/all_to_all | solution.py:65
  119.4 1.5 convolution_convert_fusion
  120.9 1.6 reshape.67
  122.5 25.1 %all-to-all-done = bf16[128,2,768]{2,1,0:T(2,128)(2,1)S(1)} async-done(((bf16[128,2,768]{2,1,0:T(2,128)(2,1)}), bf16[128,2,768]{2,1,0:T(2,128)(2,1)S(1)}, u32[]{:S(2)}, u32[]{:S(2)}) %all-to-all-start) | async-done | bytes 393248 | tf_op jit(solution)/shard_map/all_to_all | solution.py:65
  147.6 6.1 %all-to-all-start.1 = ((bf16[128,2,2048]{2,1,0:T(2,128)(2,1)}), bf16[128,2,2048]{2,1,0:T(2,128)(2,1)S(1)}, u32[]{:S(2)}, u32[]{:S(2)}) async-start(bf16[128,2,2048]{2,1,0:T(2,128)(2,1)} %reshape.67), calls=%async_computation.1 | async-start | bytes 2097152 | tf_op jit(solution)/shard_map/all_to_all | solution.py:58
  153.9 1.0 reshape.73
  154.9 54.4 %all-to-all-done.1 = bf16[128,2,2048]{2,1,0:T(2,128)(2,1)S(1)} async-done(((bf16[128,2,2048]{2,1,0:T(2,128)(2,1)}), bf16[128,2,2048]{2,1,0:T(2,128)(2,1)S(1)}, u32[]{:S(2)}, u32[]{:S(2)}) %all-to-all-start.1) | async-done | bytes 1048608 | tf_op jit(solution)/shard_map/all_to_all | solution.py:58
  209.3 1.3 reshape.68
  210.6 12.7 %fusion.40 = (bf16[1,2048,768]{2,0,1:T(2,128)(2,1)S(1)}, bf16[1,2048,768]{2,0,1:T(2,128)(2,1)S(1)}) fusion(bf16[2,2048,768]{2,0,1:T(2,128)(2,1)} %all-gather.4.cloned.1.call-done), kind=kLoop, calls=%fused_computation.69 | loop fusion | bytes 12582912 | tf_op jit(solution)/shard_map/slice | solution.py:85
  223.3 1.8 multiply_convert_fusion.1
  225.1 1.9 fusion.17
  227.1 0.7 all-gather.8.cloned.1.call-update
  227.8 1.4 fusion.41
  229.2 1.6 squeeze.15
  230.9 21.3 %all-gather.6.cloned.1.call-done = bf16[1024,768]{1,0:T(8,128)(2,1)} async-done(((bf16[256,768]{1,0:T(8,128)(2,1)}), bf16[1024,768]{1,0:T(8,128)(2,1)}) %all-gather.6.cloned.1.call-update) | async-done | bytes 1572880 | tf_op jit(solution)/shard_map/all_gather | solution.py:92
  252.3 3.8 fusion.42
  256.0 33.1 %all-gather.8.cloned.1.call-done = bf16[1024,768]{1,0:T(8,128)(2,1)} async-done(((bf16[256,768]{1,0:T(8,128)(2,1)}), bf16[1024,768]{1,0:T(8,128)(2,1)}) %all-gather.8.cloned.1.call-update) | async-done | bytes 1572880 | tf_op jit(solution)/shard_map/all_gather | solution.py:93
  289.1 4.1 add_convert_fusion.1
  293.2 3.5 all-to-all-start.3
  296.7 1.5 reshape_reshape.3
  298.2 2.4 copy.31
  300.6 10.4 %all-to-all-done.3 = bf16[4,256,512]{2,1,0:T(8,128)(2,1)S(1)} async-done(((bf16[4,256,512]{2,1,0:T(8,128)(2,1)}), bf16[4,256,512]{2,1,0:T(8,128)(2,1)S(1)}, u32[]{:S(2)}, u32[]{:S(2)}) %all-to-all-start.3) | async-done | bytes 1048608 | tf_op jit(solution)/shard_map/all_to_all | solution.py:119
  311.0 3.5 all-to-all-start.5
  314.6 1.8 copy.30
  316.3 2.3 reshape.71
  318.6 9.4 %all-to-all-done.5 = bf16[256,4,512]{2,0,1:T(8,128)(2,1)S(1)} async-done(((bf16[256,4,512]{2,0,1:T(8,128)(2,1)}), bf16[256,4,512]{2,0,1:T(8,128)(2,1)S(1)}, u32[]{:S(2)}, u32[]{:S(2)}) %all-to-all-start.5) | async-done | bytes 1048608 | tf_op jit(solution)/shard_map/all_to_all | solution.py:96
  328.0 18.6 %all-to-all-start.4 = ((bf16[128,2,2048]{2,1,0:T(2,128)(2,1)}), bf16[128,2,2048]{2,1,0:T(2,128)(2,1)S(1)}, u32[]{:S(2)}, u32[]{:S(2)}) async-start(bf16[128,2,2048]{2,1,0:T(2,128)(2,1)} %reshape.71), calls=%async_computation.4 | async-start | bytes 2097152 | tf_op jit(solution)/shard_map/all_to_all | solution.py:126
  346.6 1.4 fusion.12
  348.0 1.4 fusion.13
  349.6 1.2 copy-done.2
  351.9 0.4 fusion.6
  353.9 2.0 add_convert_fusion
  355.8 2.9 convert_element_type.82
  358.7 1.7 copy.32
  360.4 41.8 %all-to-all-done.4 = bf16[128,2,2048]{2,1,0:T(2,128)(2,1)S(1)} async-done(((bf16[128,2,2048]{2,1,0:T(2,128)(2,1)}), bf16[128,2,2048]{2,1,0:T(2,128)(2,1)S(1)}, u32[]{:S(2)}, u32[]{:S(2)}) %all-to-all-start.4) | async-done | bytes 1048608 | tf_op jit(solution)/shard_map/all_to_all | solution.py:126
  402.2 6.5 %all-to-all-start.6 = ((bf16[2,128,4,768]{3,2,0,1:T(4,128)(2,1)}), bf16[2,128,4,768]{3,2,0,1:T(4,128)(2,1)S(1)}, u32[]{:S(2)}, u32[]{:S(2)}) async-start(bf16[2,128,4,768]{3,2,0,1:T(4,128)(2,1)} %copy.32), calls=%async_computation.6 | async-start | bytes 3145728 | tf_op jit(solution)/shard_map/all_to_all | solution.py:111
  408.7 1.2 reshape.72
  410.0 2.4 convolution_convert_fusion.1
  412.4 73.8 %all-to-all-done.6 = bf16[2,128,4,768]{3,2,0,1:T(4,128)(2,1)S(1)} async-done(((bf16[2,128,4,768]{3,2,0,1:T(4,128)(2,1)}), bf16[2,128,4,768]{3,2,0,1:T(4,128)(2,1)S(1)}, u32[]{:S(2)}, u32[]{:S(2)}) %all-to-all-start.6) | async-done | bytes 1572896 | tf_op jit(solution)/shard_map/all_to_all | solution.py:111
  486.2 0.5 multiply_convert_fusion
  486.8 1.5 copy.34
  (38 shorter events, 4.0 us)
Async XLA Ops:
  7.2 1.1 copy-start
  7.2 203.4 %all-gather.4.cloned.1.call-start = ((), (), s32[]{:S(2)}) async-start(), calls=%async_computation.7 | async-start | bytes 7864320 | tf_op jit(solution)/shard_map/all_gather | solution.py:84
  110.0 0.7 copy-start.7
  110.0 1.1 copy-start.6
  110.0 1.1 copy-start.9
  112.3 35.2 %all-to-all-start = ((bf16[128,2,768]{2,1,0:T(2,128)(2,1)}), bf16[128,2,768]{2,1,0:T(2,128)(2,1)S(1)}, u32[]{:S(2)}, u32[]{:S(2)}) async-start(bf16[128,2,768]{2,1,0:T(2,128)(2,1)} %reshape.66), calls=%async_computation | async-start | bytes 786432 | tf_op jit(solution)/shard_map/all_to_all | solution.py:65
  147.6 61.7 %all-to-all-start.1 = ((bf16[128,2,2048]{2,1,0:T(2,128)(2,1)}), bf16[128,2,2048]{2,1,0:T(2,128)(2,1)S(1)}, u32[]{:S(2)}, u32[]{:S(2)}) async-start(bf16[128,2,2048]{2,1,0:T(2,128)(2,1)} %reshape.67), calls=%async_computation.1 | async-start | bytes 2097152 | tf_op jit(solution)/shard_map/all_to_all | solution.py:58
  153.7 98.6 %all-gather.6.cloned.1.call-start = ((), (), s32[]{:S(2)}) async-start(), calls=%async_computation.8 | async-start | bytes 1966080 | tf_op jit(solution)/shard_map/all_gather | solution.py:92
  210.6 12.7 %copy-start.5 = (f32[256,768]{1,0:T(8,128)S(1)}, f32[256,768]{1,0:T(8,128)}, u32[]{:S(2)}) copy-start(f32[256,768]{1,0:T(8,128)} %reshape.73) | copy-start | bytes 2359300
  210.6 12.7 %copy-start.4 = (bf16[256,2048]{1,0:T(8,128)(2,1)S(1)}, bf16[256,2048]{1,0:T(8,128)(2,1)}, u32[]{:S(2)}) copy-start(bf16[256,2048]{1,0:T(8,128)(2,1)} %reshape.68) | copy-start | bytes 3145732
  227.0 62.1 %all-gather.8.cloned.1.call-start = ((), (), s32[]{:S(2)}) async-start(), calls=%async_computation.9 | async-start | bytes 1966080 | tf_op jit(solution)/shard_map/all_gather | solution.py:93
  293.2 17.8 %all-to-all-start.3 = ((bf16[4,256,512]{2,1,0:T(8,128)(2,1)}), bf16[4,256,512]{2,1,0:T(8,128)(2,1)S(1)}, u32[]{:S(2)}, u32[]{:S(2)}) async-start(bf16[4,256,512]{2,1,0:T(8,128)(2,1)} %bitcast.99), calls=%async_computation.3 | async-start | bytes 2097152 | tf_op jit(solution)/shard_map/all_to_all | solution.py:119
  311.0 17.0 %all-to-all-start.5 = ((bf16[256,4,512]{2,0,1:T(8,128)(2,1)}), bf16[256,4,512]{2,0,1:T(8,128)(2,1)S(1)}, u32[]{:S(2)}, u32[]{:S(2)}) async-start(bf16[256,4,512]{2,0,1:T(8,128)(2,1)} %copy.31), calls=%async_computation.5 | async-start | bytes 2097152 | tf_op jit(solution)/shard_map/all_to_all | solution.py:96
  328.0 74.2 %all-to-all-start.4 = ((bf16[128,2,2048]{2,1,0:T(2,128)(2,1)}), bf16[128,2,2048]{2,1,0:T(2,128)(2,1)S(1)}, u32[]{:S(2)}, u32[]{:S(2)}) async-start(bf16[128,2,2048]{2,1,0:T(2,128)(2,1)} %reshape.71), calls=%async_computation.4 | async-start | bytes 2097152 | tf_op jit(solution)/shard_map/all_to_all | solution.py:126
  349.5 1.4 copy-start.2
  349.5 1.9 copy-start.3
  402.2 84.0 %all-to-all-start.6 = ((bf16[2,128,4,768]{3,2,0,1:T(4,128)(2,1)}), bf16[2,128,4,768]{3,2,0,1:T(4,128)(2,1)S(1)}, u32[]{:S(2)}, u32[]{:S(2)}) async-start(bf16[2,128,4,768]{3,2,0,1:T(4,128)(2,1)} %copy.32), calls=%async_computation.6 | async-start | bytes 3145728 | tf_op jit(solution)/shard_map/all_to_all | solution.py:111
  408.7 77.5 %copy-start.8 = (s32[128]{0:T(128)S(1)}, s32[128]{0:T(128)}, u32[]{:S(2)}) copy-start(s32[128]{0:T(128)} %param.10) | copy-start | bytes 1540
  410.0 78.3 %copy-start.1 = (bf16[64,2,4,768]{3,2,1,0:T(4,128)(2,1)S(1)}, bf16[64,2,4,768]{3,2,1,0:T(4,128)(2,1)}, u32[]{:S(2)}) copy-start(bf16[64,2,4,768]{3,2,1,0:T(4,128)(2,1)} %param.11) | copy-start | bytes 2359300
Sparse Core Ops, SparseCore 0:
  110.1 64.8 all-gather.3
  227.1 25.0 all-gather.5
  254.9 34.1 all-gather.7
where the time goes:
time: 496 us; the launch traced here: 495 us
  waiting for transfers between devices  270 us (54%)
  blocking collectives  96.8 us (20%)
  starting transfers between devices  45.6 us (9%)
  local copies, waits for them, and re-layouts  42.5 us (9%)
  matrix products  22.8 us (5%)
  between operations  14 us (3%)
    all_to_all x1, blocking collectives, per_device(): lax.all_to_all(send_weights, 'expert', split_axis=0, concat_axis=2, tiled...  96.8 us
    all_to_all x1, waiting for transfers between devices, per_device(): lax.all_to_all(pieces.astype(jnp.bfloat16), 'expert', split_axis=1, conca...  73.8 us
    all_to_all x1, waiting for transfers between devices, per_device(): lax.all_to_all(send_inputs.reshape(expert_count, capacity, model_width),...  54.4 us
    all_to_all x1, waiting for transfers between devices, per_device(): lax.all_to_all(joined.reshape(expert_count, capacity, model_width), 'expe...  41.8 us
    all_gather x1, waiting for transfers between devices, per_device(): lax.all_gather(grad_up, 'dp', axis=0, tiled=True)  33.1 us
    all_to_all x1, waiting for transfers between devices, per_device(): lax.all_to_all(send_cotangent.reshape(expert_count, capacity, hidden_widt...  25.1 us
    all_gather x1, waiting for transfers between devices, per_device(): lax.all_gather(grad_gate, 'dp', axis=0, tiled=True)  21.3 us
    all_to_all x1, starting transfers between devices, per_device(): lax.all_to_all(joined.reshape(expert_count, capacity, model_width), 'expe...  18.6 us
  transfers between devices with their start and end apart: 9, of which 8 were waited for; matrix products, arithmetic and copies ran while one was open for 8% of the time, Pallas kernels for 0%

commit v1 on v0

--- a/solution.py
+++ b/solution.py
@@ -88,9 +88,22 @@
     scaled = recv_cotangent.astype(jnp.float32)
     grad_gate = (scaled * up_sum * sigma * (1.0 + gate_sum * (1.0 - sigma))).astype(jnp.bfloat16)
     grad_up = (scaled * gate_sum * sigma).astype(jnp.bfloat16)
+
+    def arrange_frame_on(x_part):
+        out_arr = jnp.concatenate(
+            jax.lax.all_to_all(
+                jnp.stack(tuple((x_part for _ in range(jax.lax.axis_size("dp")))), 0),
+                "dp",
+                split_axis=0,
+                concat_axis=0,
+            ),
+            0,
+        )
+        return out_arr
+
     all_gate, all_up = (
         lax.all_gather(grad_gate, "dp", axis=0, tiled=True),
-        lax.all_gather(grad_up, "dp", axis=0, tiled=True),
+        arrange_frame_on(grad_up),
     )
     split_inputs = recv_inputs.reshape(depth_rows, group_count, block_rows)
     all_columns = lax.all_to_all(

time: 496 us -> 469 us (0.946)
  waiting for transfers between devices: 270 us -> 242 us
    all_gather x1 -> x0, waiting for transfers between devices: 33.1 us -> none  [per_device(): lax.all_gather(grad_up, 'dp', axis=0, tiled=True)]
    all_to_all x1, starting transfers between devices: 18.6 us -> 10.9 us  [per_device(): lax.all_to_all(joined.reshape(expert_count, capacity, model_width), 'expe...]
    all_gather x1, waiting for transfers between devices: 21.3 us -> 28.1 us  [per_device(): lax.all_gather(grad_gate, 'dp', axis=0, tiled=True)]
  transfers between devices with their start and end apart: 9 -> 9, of which waited for: 8 -> 7; matrix products, arithmetic and copies ran while one was open for 8% -> 9% of each run, Pallas kernels for 0% -> 0%
where the time goes in v1:
time: 469 us; the launch traced here: 468 us
  waiting for transfers between devices  242 us (52%)
  blocking collectives  96.8 us (21%)
  local copies, waits for them, and re-layouts  43.5 us (9%)
  starting transfers between devices  43 us (9%)
  matrix products  24.9 us (5%)
  between operations  14.3 us (3%)
    all_to_all x1, blocking collectives, per_device(): lax.all_to_all(send_weights, 'expert', split_axis=0, concat_axis=2, tiled...  96.8 us
    all_to_all x1, waiting for transfers between devices, per_device(): lax.all_to_all(pieces.astype(jnp.bfloat16), 'expert', split_axis=1, conca...  73.8 us
    all_to_all x1, waiting for transfers between devices, per_device(): lax.all_to_all(send_inputs.reshape(expert_count, capacity, model_width),...  54.4 us
    all_to_all x1, waiting for transfers between devices, per_device(): lax.all_to_all(joined.reshape(expert_count, capacity, model_width), 'expe...  40.9 us
    all_gather x1, waiting for transfers between devices, per_device(): lax.all_gather(grad_gate, 'dp', axis=0, tiled=True)  28.1 us
    all_to_all x1, waiting for transfers between devices, per_device(): lax.all_to_all(send_cotangent.reshape(expert_count, capacity, hidden_widt...  25.1 us
    slice x1, local copies, waits for them, and re-layouts, per_device(): piece[0]  12.7 us
    all_to_all x1, starting transfers between devices, per_device(): lax.all_to_all(joined.reshape(expert_count, capacity, model_width), 'expe...  10.9 us
  transfers between devices with their start and end apart: 9, of which 7 were waited for; matrix products, arithmetic and copies ran while one was open for 9% of the time, Pallas kernels for 0%

profile of v1, /device:TPU:33, one launch (start us, length us, event | category | flops | bytes accessed | tf_op | source)
XLA Modules:
  0.0 467.8 jit_solution(17639101478171728347)
XLA Ops:
  7.2 1.1 copy-done
  8.3 1.3 convolution_convert_fusion.2
  9.6 1.2 copy.26
  10.8 96.8 %all_to_all.70 = bf16[128,2,4,768]{3,2,1,0:T(4,128)(2,1)S(1)} all-to-all(bf16[128,2,4,768]{3,2,1,0:T(4,128)(2,1)S(1)} %copy.26), channel_id=1, replica_groups=mesh['dp'=4,'expert'=128] {'expert'}, dimensions={0} | all-to-all | bytes 3145728 | tf_op jit(solution)/shard_map/all_to_all | solution.py:81
  107.6 2.4 copy.27
  110.0 0.6 copy-done.6
  111.4 0.9 reshape.75
  112.3 7.0 %all-to-all-start = ((bf16[128,2,768]{2,1,0:T(2,128)(2,1)}), bf16[128,2,768]{2,1,0:T(2,128)(2,1)S(1)}, u32[]{:S(2)}, u32[]{:S(2)}) async-start(bf16[128,2,768]{2,1,0:T(2,128)(2,1)} %reshape.75), calls=%async_computation | async-start | bytes 786432 | tf_op jit(solution)/shard_map/all_to_all | solution.py:65
  119.4 1.5 convolution_convert_fusion
  120.9 1.6 reshape.76
  122.5 25.1 %all-to-all-done = bf16[128,2,768]{2,1,0:T(2,128)(2,1)S(1)} async-done(((bf16[128,2,768]{2,1,0:T(2,128)(2,1)}), bf16[128,2,768]{2,1,0:T(2,128)(2,1)S(1)}, u32[]{:S(2)}, u32[]{:S(2)}) %all-to-all-start) | async-done | bytes 393248 | tf_op jit(solution)/shard_map/all_to_all | solution.py:65
  147.6 6.1 %all-to-all-start.1 = ((bf16[128,2,2048]{2,1,0:T(2,128)(2,1)}), bf16[128,2,2048]{2,1,0:T(2,128)(2,1)S(1)}, u32[]{:S(2)}, u32[]{:S(2)}) async-start(bf16[128,2,2048]{2,1,0:T(2,128)(2,1)} %reshape.76), calls=%async_computation.1 | async-start | bytes 2097152 | tf_op jit(solution)/shard_map/all_to_all | solution.py:58
  153.9 1.0 reshape.83
  154.9 54.4 %all-to-all-done.1 = bf16[128,2,2048]{2,1,0:T(2,128)(2,1)S(1)} async-done(((bf16[128,2,2048]{2,1,0:T(2,128)(2,1)}), bf16[128,2,2048]{2,1,0:T(2,128)(2,1)S(1)}, u32[]{:S(2)}, u32[]{:S(2)}) %all-to-all-start.1) | async-done | bytes 1048608 | tf_op jit(solution)/shard_map/all_to_all | solution.py:58
  209.3 1.3 reshape.77
  210.5 12.7 %fusion.36 = (bf16[1,2048,768]{2,0,1:T(2,128)(2,1)S(1)}, bf16[1,2048,768]{2,0,1:T(2,128)(2,1)S(1)}) fusion(bf16[2,2048,768]{2,0,1:T(2,128)(2,1)} %all-gather.3.cloned.1.call-done), kind=kLoop, calls=%fused_computation.69 | loop fusion | bytes 12582912 | tf_op jit(solution)/shard_map/slice | solution.py:85
  223.3 1.8 multiply_convert_fusion.1
  225.1 1.9 fusion.17
  227.0 2.3 stack.55
  229.3 4.3 all-to-all-start.3
  233.6 1.4 fusion.37
  235.1 1.6 squeeze.15
  236.8 28.1 %all-gather.5.cloned.1.call-done = bf16[1024,768]{1,0:T(8,128)(2,1)} async-done(((bf16[256,768]{1,0:T(8,128)(2,1)}), bf16[1024,768]{1,0:T(8,128)(2,1)}) %all-gather.5.cloned.1.call-update) | async-done | bytes 1572880 | tf_op jit(solution)/shard_map/all_gather | solution.py:105
  264.9 3.7 fusion.38
  268.6 4.1 add_convert_fusion.1
  272.7 4.4 all-to-all-start.4
  277.1 1.5 reshape_reshape.3
  278.5 2.4 copy.31
  281.0 10.4 %all-to-all-done.4 = bf16[4,256,512]{2,1,0:T(8,128)(2,1)S(1)} async-done(((bf16[4,256,512]{2,1,0:T(8,128)(2,1)}), bf16[4,256,512]{2,1,0:T(8,128)(2,1)S(1)}, u32[]{:S(2)}, u32[]{:S(2)}) %all-to-all-start.4) | async-done | bytes 1048608 | tf_op jit(solution)/shard_map/all_to_all | solution.py:132
  291.4 3.5 all-to-all-start.6
  294.9 1.8 copy.30
  296.7 2.3 reshape.81
  299.0 9.4 %all-to-all-done.6 = bf16[256,4,512]{2,0,1:T(8,128)(2,1)S(1)} async-done(((bf16[256,4,512]{2,0,1:T(8,128)(2,1)}), bf16[256,4,512]{2,0,1:T(8,128)(2,1)S(1)}, u32[]{:S(2)}, u32[]{:S(2)}) %all-to-all-start.6) | async-done | bytes 1048608 | tf_op jit(solution)/shard_map/all_to_all | solution.py:109
  308.4 10.9 %all-to-all-start.5 = ((bf16[128,2,2048]{2,1,0:T(2,128)(2,1)}), bf16[128,2,2048]{2,1,0:T(2,128)(2,1)S(1)}, u32[]{:S(2)}, u32[]{:S(2)}) async-start(bf16[128,2,2048]{2,1,0:T(2,128)(2,1)} %reshape.81), calls=%async_computation.5 | async-start | bytes 2097152 | tf_op jit(solution)/shard_map/all_to_all | solution.py:139
  319.3 1.4 fusion.13
  320.7 1.4 fusion.11
  322.1 1.5 fusion.9
  323.7 1.4 fusion.7
  327.3 2.0 add_convert_fusion
  329.3 2.9 convert_element_type.82
  332.2 1.7 copy.32
  333.9 40.9 %all-to-all-done.5 = bf16[128,2,2048]{2,1,0:T(2,128)(2,1)S(1)} async-done(((bf16[128,2,2048]{2,1,0:T(2,128)(2,1)}), bf16[128,2,2048]{2,1,0:T(2,128)(2,1)S(1)}, u32[]{:S(2)}, u32[]{:S(2)}) %all-to-all-start.5) | async-done | bytes 1048608 | tf_op jit(solution)/shard_map/all_to_all | solution.py:139
  374.9 6.5 %all-to-all-start.7 = ((bf16[2,128,4,768]{3,2,0,1:T(4,128)(2,1)}), bf16[2,128,4,768]{3,2,0,1:T(4,128)(2,1)S(1)}, u32[]{:S(2)}, u32[]{:S(2)}) async-start(bf16[2,128,4,768]{3,2,0,1:T(4,128)(2,1)} %copy.32), calls=%async_computation.7 | async-start | bytes 3145728 | tf_op jit(solution)/shard_map/all_to_all | solution.py:124
  381.4 1.2 reshape.82
  382.6 2.4 convolution_convert_fusion.1
  385.1 73.8 %all-to-all-done.7 = bf16[2,128,4,768]{3,2,0,1:T(4,128)(2,1)S(1)} async-done(((bf16[2,128,4,768]{3,2,0,1:T(4,128)(2,1)}), bf16[2,128,4,768]{3,2,0,1:T(4,128)(2,1)S(1)}, u32[]{:S(2)}, u32[]{:S(2)}) %all-to-all-start.7) | async-done | bytes 1572896 | tf_op jit(solution)/shard_map/all_to_all | solution.py:124
  458.9 0.5 multiply_convert_fusion
  459.4 1.5 copy.34
  (36 shorter events, 3.5 us)
Async XLA Ops:
  7.2 1.1 copy-start
  7.2 203.4 %all-gather.3.cloned.1.call-start = ((), (), s32[]{:S(2)}) async-start(), calls=%async_computation.8 | async-start | bytes 7864320 | tf_op jit(solution)/shard_map/all_gather | solution.py:84
  110.0 0.7 copy-start.6
  110.0 1.1 copy-start.5
  110.0 1.1 copy-start.8
  112.3 35.2 %all-to-all-start = ((bf16[128,2,768]{2,1,0:T(2,128)(2,1)}), bf16[128,2,768]{2,1,0:T(2,128)(2,1)S(1)}, u32[]{:S(2)}, u32[]{:S(2)}) async-start(bf16[128,2,768]{2,1,0:T(2,128)(2,1)} %reshape.75), calls=%async_computation | async-start | bytes 786432 | tf_op jit(solution)/shard_map/all_to_all | solution.py:65
  147.6 61.7 %all-to-all-start.1 = ((bf16[128,2,2048]{2,1,0:T(2,128)(2,1)}), bf16[128,2,2048]{2,1,0:T(2,128)(2,1)S(1)}, u32[]{:S(2)}, u32[]{:S(2)}) async-start(bf16[128,2,2048]{2,1,0:T(2,128)(2,1)} %reshape.76), calls=%async_computation.1 | async-start | bytes 2097152 | tf_op jit(solution)/shard_map/all_to_all | solution.py:58
  153.7 111.2 %all-gather.5.cloned.1.call-start = ((), (), s32[]{:S(2)}) async-start(), calls=%async_computation.9 | async-start | bytes 1966080 | tf_op jit(solution)/shard_map/all_gather | solution.py:105
  210.5 12.8 %copy-start.4 = (f32[256,768]{1,0:T(8,128)S(1)}, f32[256,768]{1,0:T(8,128)}, u32[]{:S(2)}) copy-start(f32[256,768]{1,0:T(8,128)} %reshape.83) | copy-start | bytes 2359300
  210.5 12.8 %copy-start.3 = (bf16[256,2048]{1,0:T(8,128)(2,1)S(1)}, bf16[256,2048]{1,0:T(8,128)(2,1)}, u32[]{:S(2)}) copy-start(bf16[256,2048]{1,0:T(8,128)(2,1)} %reshape.77) | copy-start | bytes 3145732
  229.3 39.4 %all-to-all-start.3 = ((bf16[4,256,768]{2,1,0:T(8,128)(2,1)}), bf16[4,256,768]{2,1,0:T(8,128)(2,1)}, u32[]{:S(2)}, u32[]{:S(2)}) async-start(bf16[4,256,768]{2,1,0:T(8,128)(2,1)} %stack.55), calls=%async_computation.3 | async-start | bytes 3145728 | tf_op jit(solution)/shard_map/all_to_all | solution.py:94
  272.7 18.7 %all-to-all-start.4 = ((bf16[4,256,512]{2,1,0:T(8,128)(2,1)}), bf16[4,256,512]{2,1,0:T(8,128)(2,1)S(1)}, u32[]{:S(2)}, u32[]{:S(2)}) async-start(bf16[4,256,512]{2,1,0:T(8,128)(2,1)} %bitcast.112), calls=%async_computation.4 | async-start | bytes 2097152 | tf_op jit(solution)/shard_map/all_to_all | solution.py:132
  291.4 17.0 %all-to-all-start.6 = ((bf16[256,4,512]{2,0,1:T(8,128)(2,1)}), bf16[256,4,512]{2,0,1:T(8,128)(2,1)S(1)}, u32[]{:S(2)}, u32[]{:S(2)}) async-start(bf16[256,4,512]{2,0,1:T(8,128)(2,1)} %copy.31), calls=%async_computation.6 | async-start | bytes 2097152 | tf_op jit(solution)/shard_map/all_to_all | solution.py:109
  308.4 66.5 %all-to-all-start.5 = ((bf16[128,2,2048]{2,1,0:T(2,128)(2,1)}), bf16[128,2,2048]{2,1,0:T(2,128)(2,1)S(1)}, u32[]{:S(2)}, u32[]{:S(2)}) async-start(bf16[128,2,2048]{2,1,0:T(2,128)(2,1)} %reshape.81), calls=%async_computation.5 | async-start | bytes 2097152 | tf_op jit(solution)/shard_map/all_to_all | solution.py:139
  322.1 2.9 copy-start.2
  374.9 84.0 %all-to-all-start.7 = ((bf16[2,128,4,768]{3,2,0,1:T(4,128)(2,1)}), bf16[2,128,4,768]{3,2,0,1:T(4,128)(2,1)S(1)}, u32[]{:S(2)}, u32[]{:S(2)}) async-start(bf16[2,128,4,768]{3,2,0,1:T(4,128)(2,1)} %copy.32), calls=%async_computation.7 | async-start | bytes 3145728 | tf_op jit(solution)/shard_map/all_to_all | solution.py:124
  381.4 77.5 %copy-start.7 = (s32[128]{0:T(128)S(1)}, s32[128]{0:T(128)}, u32[]{:S(2)}) copy-start(s32[128]{0:T(128)} %param.10) | copy-start | bytes 1540
  382.6 78.3 %copy-start.1 = (bf16[64,2,4,768]{3,2,1,0:T(4,128)(2,1)S(1)}, bf16[64,2,4,768]{3,2,1,0:T(4,128)(2,1)}, u32[]{:S(2)}) copy-start(bf16[64,2,4,768]{3,2,1,0:T(4,128)(2,1)} %param.11) | copy-start | bytes 2359300
Sparse Core Ops, SparseCore 0:
  110.1 64.8 all-gather.2
  227.1 37.7 all-gather.4
